TPU v7x, 32 devices: a whole 2x2x4 slice. The times are simulated.
32 devices in a mesh: gx: 4 (over z), gy: 2 (over y), gz: 4 (over x, core).
Axes of the slice: x: 2, y: 2, z: 4, core: 2. Of those that a mesh axis runs over, the one named last changes fastest.
Arguments:
- bodies: float32 [1920, 4, 128], P(('gx', 'gy', 'gz'))
- velocity: float32 [1920, 3, 128], P(('gx', 'gy', 'gz')), may hold values from -6 to 6
- select: int32 [32, 5, 16], P(('gx', 'gy', 'gz')), may hold values from 0 to 123, as said below
- pair_target: int32 [32, 1024], P(('gx', 'gy', 'gz')), may hold values from 0 to 59
- pair_source: int32 [32, 1024], P(('gx', 'gy', 'gz')), may hold values from 0 to 139
- counts: int32 [32], P(('gx', 'gy', 'gz')), may hold values from 256 to 1024, as said below
- departures: int32 [32, 12], P(('gx', 'gy', 'gz')), may hold values from 0 to 59, as said below
- owners: int32 [384, 1], P(('gx', 'gy', 'gz')), may hold values from 0 to 3; in each aligned block of 12 rows (0 to 11, 12 to 23, ...) at most 6 rows name the same one
Outputs:
- resident: float32 [1920, 7, 128], P(('gx', 'gy', 'gz'))
- moved_in: float32 [768, 7, 128], P(('gx', 'gy', 'gz'))
Inputs may be any that keep to these rules, and one draw needn't show every extreme that they name: `select`: at step k every entry is below 60 + k * 16, and each list names the block 60 + k * 16 - 1. `counts`: some device has 1024 live pairs. `departures`: entries of one device are distinct. `owners`: no owner gets more than 6 blocks from one device, and that many in some devices.
All inputs are finite; a program needn't handle non-finite values.
Results may differ from a plain program's by a relative error of at most 0.0003.
Values sent between devices are 32-bit elements; how exact they have to be, the bound alone decides.
A program may use at most 64 MiB of HBM per device.

v0:
```python
import jax
import jax.numpy as jnp
from jax import lax
from jax.sharding import PartitionSpec as P

soften = 0.01
timestep = 0.25
group_rows = 64


def swapped(value, axis, stride):
    mask = 2**stride
    pairs = [(source, source ^ mask) for source in range(lax.axis_size(axis))]
    return lax.ppermute(value, axis, pairs)


def block_forces(targets, sources, validity):
    delta_x = sources[:, 0, None, :] - targets[:, 0, :, None]
    offset_vertical = sources[:, 1, None, :] - targets[:, 1, :, None]
    delta_z = sources[:, 2, None, :] - targets[:, 2, :, None]
    radius_sq = delta_x * delta_x + offset_vertical * offset_vertical + delta_z * delta_z + soften
    weight = sources[:, 3, None, :] * lax.rsqrt(radius_sq) / radius_sq
    pull_sums = jnp.stack(
        [
            jnp.sum(delta_x * weight, axis=2),
            jnp.sum(offset_vertical * weight, axis=2),
            jnp.sum(delta_z * weight, axis=2),
        ],
        axis=1,
    )
    return pull_sums * validity[:, None, None]


def on_device(bodies, velocity, select, pair_target, pair_source, counts, departures, owners):
    own_blocks = bodies.shape[0]
    block_span_rows = bodies.shape[2]
    send_count = select.shape[2]
    pair_total = pair_target.shape[1]
    bits_gx = lax.axis_size("gx").bit_length() - 1
    bits_gy = lax.axis_size("gy").bit_length() - 1
    bits_gz = lax.axis_size("gz").bit_length() - 1
    pool_size = own_blocks + send_count * (bits_gx + bits_gy + bits_gz)
    holdings = jnp.zeros((pool_size, 4, block_span_rows), jnp.float32).at[:own_blocks].set(bodies)
    targets = pair_target[0]
    sources = pair_source[0]
    pair_limit = counts[0]
    positions = jnp.arange(pair_total, dtype=jnp.int32)
    in_range = positions < pair_limit
    ordering = jnp.argsort(jnp.where(in_range, sources, pool_size + positions), stable=True)
    sorted_target = targets[ordering]
    sorted_source = sources[ordering]
    members = jnp.arange(own_blocks, dtype=jnp.int32)

    def extend(pool_now, step_index, incoming):
        lower_block = own_blocks + send_count * step_index
        return pool_now.at[lower_block : lower_block + send_count].set(incoming)

    zero_accel = jnp.zeros((own_blocks, 3, block_span_rows), jnp.float32)
    step_index = 0
    for bit_index in range(bits_gx):
        incoming = swapped(holdings[select[0, step_index]], "gx", bit_index)
        holdings = extend(holdings, step_index, incoming)
        step_index = step_index + 1
    for bit_index in range(bits_gy):
        incoming = swapped(holdings[select[0, step_index]], "gy", bit_index)
        holdings = extend(holdings, step_index, incoming)
        step_index = step_index + 1
    for bit_index in range(bits_gz):
        incoming = swapped(holdings[select[0, step_index]], "gz", bit_index)
        holdings = extend(holdings, step_index, incoming)
        step_index = step_index + 1
    pool_now = holdings

    def add_group(group_index, partial_value):
        first_row = group_index * group_rows
        target_rows = lax.dynamic_slice_in_dim(sorted_target, first_row, group_rows)
        source_rows = lax.dynamic_slice_in_dim(sorted_source, first_row, group_rows)
        offsets = first_row + jnp.arange(group_rows, dtype=jnp.int32)
        validity = ((offsets >= 0) & (offsets < pair_limit)).astype(jnp.float32)
        pull_sums = block_forces(bodies[target_rows], pool_now[source_rows], validity)
        onehot = (target_rows[:, None] == members[None, :]).astype(jnp.float32)
        return partial_value + jnp.einsum(
            "gk,gcb->kcb", onehot, pull_sums, precision=lax.Precision.HIGHEST
        )

    accelerations = lax.fori_loop(
        0 // group_rows, (pair_limit + group_rows - 1) // group_rows, add_group, zero_accel
    )
    velocity_new = velocity + timestep * accelerations
    position = bodies[:, :3, :] + timestep * velocity_new
    refreshed_state = jnp.concatenate([position, bodies[:, 3:4, :], velocity_new], axis=1)
    departing_body_index = departures[0]
    move_count = departing_body_index.shape[0]
    group_size = lax.axis_size("gz")
    slot_total = max(2, 2 * move_count // group_size)
    departed = jnp.any(members[:, None] == departing_body_index[None, :], axis=1)
    resident = jnp.where(departed[:, None, None], jnp.zeros_like(refreshed_state), refreshed_state)
    owner_rows = owners[:, 0]
    same_owner = owner_rows[:, None] == owner_rows[None, :]
    moves = jnp.arange(move_count, dtype=jnp.int32)
    prior_positions = moves[None, :] < moves[:, None]
    place_slot_index = jnp.sum((same_owner & prior_positions).astype(jnp.int32), axis=1)
    body_routes_table = (
        (owner_rows[:, None, None] == jnp.arange(group_size, dtype=jnp.int32)[None, :, None])
        & (
            place_slot_index[:, None, None]
            == jnp.arange(slot_total, dtype=jnp.int32)[None, None, :]
        )
    ).astype(jnp.float32)
    outbox = jnp.einsum(
        "awn,ajz->wnjz",
        body_routes_table,
        refreshed_state[departing_body_index],
        precision=lax.Precision.HIGHEST,
    )
    arrived = lax.all_to_all(outbox, "gz", split_axis=0, concat_axis=0, tiled=True)
    moved_in = arrived.reshape(group_size * slot_total, 7, block_span_rows)
    return (resident, moved_in)


def solution(mesh):
    return jax.shard_map(
        on_device,
        mesh=mesh,
        in_specs=(
            P(("gx", "gy", "gz"), None, None),
            P(("gx", "gy", "gz"), None, None),
            P(("gx", "gy", "gz"), None, None),
            P(("gx", "gy", "gz"), None),
            P(("gx", "gy", "gz"), None),
            P(("gx", "gy", "gz")),
            P(("gx", "gy", "gz"), None),
            P(("gx", "gy", "gz"), None),
        ),
        out_specs=(P(("gx", "gy", "gz"), None, None), P(("gx", "gy", "gz"), None, None)),
        check_vma=False,
    )
```

profile of v0, /device:TPU:4, one launch (start us, length us, event | category | flops | bytes accessed | tf_op | source)
XLA Modules:
  0.0 204.0 jit_solution(4861677650795399104)
XLA Ops:
  0.7 0.7 fusion.31
  1.4 0.9 scatter.20
  3.0 1.6 collective-permute-start
  5.5 4.4 %sort.17 = (s32[1024]{0:T(1024)}, s32[1024]{0:T(1024)S(1)}) sort(s32[1024]{0:T(1024)S(1)} %add_select_fusion, s32[1024]{0:T(1024)S(1)} %iota.45), dimensions={0}, to_apply=%region_1.2 | sort | flops 10240 | bytes 16384 | tf_op jit(solution)/shard_map/jit(argsort)/sort | solution.py:49
  10.6 2.7 %collective-permute-start.1 = (f32[16,4,128]{2,1,0:T(4,128)S(1)}, f32[16,4,128]{2,1,0:T(4,128)S(1)}, u32[]{:S(2)}, u32[]{:S(2)}) collective-permute-start(f32[16,4,128]{2,1,0:T(4,128)S(1)} %gather_fusion.5), channel_id=1, source_target_pairs={{0,16},{8,24},{16,0},{24,8},{1,17},{9,25},{17,1},{25,9},{2,18},{10... | collective-permute-start | bytes 98312 | tf_op jit(solution)/shard_map/ppermute | solution.py:14
  13.3 2.5 %collective-permute-done.1 = f32[16,4,128]{2,1,0:T(4,128)S(1)} collective-permute-done((f32[16,4,128]{2,1,0:T(4,128)S(1)}, f32[16,4,128]{2,1,0:T(4,128)S(1)}, u32[]{:S(2)}, u32[]{:S(2)}) %collective-permute-start.1) | collective-permute-done | bytes 32800 | tf_op jit(solution)/shard_map/ppermute | solution.py:14
  16.6 3.6 %collective-permute-done.2 = f32[16,4,128]{2,1,0:T(4,128)S(1)} collective-permute-done((f32[16,4,128]{2,1,0:T(4,128)S(1)}, f32[16,4,128]{2,1,0:T(4,128)S(1)}, u32[]{:S(2)}, u32[]{:S(2)}) %collective-permute-start.2) | collective-permute-done | bytes 32800 | tf_op jit(solution)/shard_map/ppermute | solution.py:14
  21.0 1.2 collective-permute-done.3
  22.7 1.6 collective-permute-start.4
  24.4 4.5 %gather_fusion.3 = s32[1024]{0:T(1024)S(1)} fusion(s32[1024]{0:T(1024)S(1)} %bitcast.78, s32[1024]{0:T(1024)S(1)} %fusion.26), kind=kCustom, calls=%fused_computation.3 | custom fusion | bytes 12288 | tf_op jit(solution)/shard_map/gather | solution.py:51
  28.9 4.5 %gather_fusion.2 = s32[1024]{0:T(1024)S(1)} fusion(s32[1024]{0:T(1024)S(1)} %bitcast.76, s32[1024]{0:T(1024)S(1)} %fusion.26), kind=kCustom, calls=%fused_computation.2 | custom fusion | bytes 12288 | tf_op jit(solution)/shard_map/gather | solution.py:50
  33.5 101.7 %while.17 = (s32[]{:T(128)}, f32[60,3,128]{2,0,1:T(8,128)S(1)}, s32[]{:T(128)}, s32[1024]{0:T(1024)S(1)}, s32[1024]{0:T(1024)S(1)}, /*index=5*/f32[140,4,128]{2,...) while((s32[]{:T(128)}, f32[60,3,128]{2,0,1:T(8,128)S(1)}, ...), condition=%wide.region_6.7_spmd.clone, body=%wide.region_2.6_spmd.clone.sunk | while | flops 35599300 | bytes 1604783 | solution.py:86
  35.2 7.6 %fusion.42 = (f32[64,128]{1,0:T(8,128)S(1)}, f32[64,128]{1,0:T(8,128)S(1)}, f32[64,128]{1,0:T(8,128)S(1)}) fusion(f32[64,128]{1,0:T(8,128)S(1)} %bitcast.84, f32[64,128]{1,0:T(8,128)S(1)} %bitcast.88, f32[64,128]{1,0:T(8,128)S(1)} %bitcast.85, f32[64,128]{1,0:T(8,128)S(1)} %bitcast.89, f32[64,128]{1,0:T(8,128)S(1)} %bitcast.83, ...), kind=kLoop, calls=%fused_computation.20.clone.1 | loop fusion | flops 17801216 | bytes 327680 | tf_op jit(solution)/shard_map/while/body/reduce_sum | solution.py:25
  45.3 7.6 %fusion.42 = (f32[64,128]{1,0:T(8,128)S(1)}, f32[64,128]{1,0:T(8,128)S(1)}, f32[64,128]{1,0:T(8,128)S(1)}) fusion(f32[64,128]{1,0:T(8,128)S(1)} %bitcast.84, f32[64,128]{1,0:T(8,128)S(1)} %bitcast.88, f32[64,128]{1,0:T(8,128)S(1)} %bitcast.85, f32[64,128]{1,0:T(8,128)S(1)} %bitcast.89, f32[64,128]{1,0:T(8,128)S(1)} %bitcast.83, ...), kind=kLoop, calls=%fused_computation.20.clone.1 | loop fusion | flops 17801216 | bytes 327680 | tf_op jit(solution)/shard_map/while/body/reduce_sum | solution.py:25
  55.5 7.6 %fusion.42 = (f32[64,128]{1,0:T(8,128)S(1)}, f32[64,128]{1,0:T(8,128)S(1)}, f32[64,128]{1,0:T(8,128)S(1)}) fusion(f32[64,128]{1,0:T(8,128)S(1)} %bitcast.84, f32[64,128]{1,0:T(8,128)S(1)} %bitcast.88, f32[64,128]{1,0:T(8,128)S(1)} %bitcast.85, f32[64,128]{1,0:T(8,128)S(1)} %bitcast.89, f32[64,128]{1,0:T(8,128)S(1)} %bitcast.83, ...), kind=kLoop, calls=%fused_computation.20.clone.1 | loop fusion | flops 17801216 | bytes 327680 | tf_op jit(solution)/shard_map/while/body/reduce_sum | solution.py:25
  65.7 7.6 %fusion.42 = (f32[64,128]{1,0:T(8,128)S(1)}, f32[64,128]{1,0:T(8,128)S(1)}, f32[64,128]{1,0:T(8,128)S(1)}) fusion(f32[64,128]{1,0:T(8,128)S(1)} %bitcast.84, f32[64,128]{1,0:T(8,128)S(1)} %bitcast.88, f32[64,128]{1,0:T(8,128)S(1)} %bitcast.85, f32[64,128]{1,0:T(8,128)S(1)} %bitcast.89, f32[64,128]{1,0:T(8,128)S(1)} %bitcast.83, ...), kind=kLoop, calls=%fused_computation.20.clone.1 | loop fusion | flops 17801216 | bytes 327680 | tf_op jit(solution)/shard_map/while/body/reduce_sum | solution.py:25
  75.9 7.6 %fusion.42 = (f32[64,128]{1,0:T(8,128)S(1)}, f32[64,128]{1,0:T(8,128)S(1)}, f32[64,128]{1,0:T(8,128)S(1)}) fusion(f32[64,128]{1,0:T(8,128)S(1)} %bitcast.84, f32[64,128]{1,0:T(8,128)S(1)} %bitcast.88, f32[64,128]{1,0:T(8,128)S(1)} %bitcast.85, f32[64,128]{1,0:T(8,128)S(1)} %bitcast.89, f32[64,128]{1,0:T(8,128)S(1)} %bitcast.83, ...), kind=kLoop, calls=%fused_computation.20.clone.1 | loop fusion | flops 17801216 | bytes 327680 | tf_op jit(solution)/shard_map/while/body/reduce_sum | solution.py:25
  86.0 7.6 %fusion.42 = (f32[64,128]{1,0:T(8,128)S(1)}, f32[64,128]{1,0:T(8,128)S(1)}, f32[64,128]{1,0:T(8,128)S(1)}) fusion(f32[64,128]{1,0:T(8,128)S(1)} %bitcast.84, f32[64,128]{1,0:T(8,128)S(1)} %bitcast.88, f32[64,128]{1,0:T(8,128)S(1)} %bitcast.85, f32[64,128]{1,0:T(8,128)S(1)} %bitcast.89, f32[64,128]{1,0:T(8,128)S(1)} %bitcast.83, ...), kind=kLoop, calls=%fused_computation.20.clone.1 | loop fusion | flops 17801216 | bytes 327680 | tf_op jit(solution)/shard_map/while/body/reduce_sum | solution.py:25
  96.2 7.6 %fusion.42 = (f32[64,128]{1,0:T(8,128)S(1)}, f32[64,128]{1,0:T(8,128)S(1)}, f32[64,128]{1,0:T(8,128)S(1)}) fusion(f32[64,128]{1,0:T(8,128)S(1)} %bitcast.84, f32[64,128]{1,0:T(8,128)S(1)} %bitcast.88, f32[64,128]{1,0:T(8,128)S(1)} %bitcast.85, f32[64,128]{1,0:T(8,128)S(1)} %bitcast.89, f32[64,128]{1,0:T(8,128)S(1)} %bitcast.83, ...), kind=kLoop, calls=%fused_computation.20.clone.1 | loop fusion | flops 17801216 | bytes 327680 | tf_op jit(solution)/shard_map/while/body/reduce_sum | solution.py:25
  106.4 7.6 %fusion.42 = (f32[64,128]{1,0:T(8,128)S(1)}, f32[64,128]{1,0:T(8,128)S(1)}, f32[64,128]{1,0:T(8,128)S(1)}) fusion(f32[64,128]{1,0:T(8,128)S(1)} %bitcast.84, f32[64,128]{1,0:T(8,128)S(1)} %bitcast.88, f32[64,128]{1,0:T(8,128)S(1)} %bitcast.85, f32[64,128]{1,0:T(8,128)S(1)} %bitcast.89, f32[64,128]{1,0:T(8,128)S(1)} %bitcast.83, ...), kind=kLoop, calls=%fused_computation.20.clone.1 | loop fusion | flops 17801216 | bytes 327680 | tf_op jit(solution)/shard_map/while/body/reduce_sum | solution.py:25
  116.5 7.6 %fusion.42 = (f32[64,128]{1,0:T(8,128)S(1)}, f32[64,128]{1,0:T(8,128)S(1)}, f32[64,128]{1,0:T(8,128)S(1)}) fusion(f32[64,128]{1,0:T(8,128)S(1)} %bitcast.84, f32[64,128]{1,0:T(8,128)S(1)} %bitcast.88, f32[64,128]{1,0:T(8,128)S(1)} %bitcast.85, f32[64,128]{1,0:T(8,128)S(1)} %bitcast.89, f32[64,128]{1,0:T(8,128)S(1)} %bitcast.83, ...), kind=kLoop, calls=%fused_computation.20.clone.1 | loop fusion | flops 17801216 | bytes 327680 | tf_op jit(solution)/shard_map/while/body/reduce_sum | solution.py:25
  126.7 7.6 %fusion.42 = (f32[64,128]{1,0:T(8,128)S(1)}, f32[64,128]{1,0:T(8,128)S(1)}, f32[64,128]{1,0:T(8,128)S(1)}) fusion(f32[64,128]{1,0:T(8,128)S(1)} %bitcast.84, f32[64,128]{1,0:T(8,128)S(1)} %bitcast.88, f32[64,128]{1,0:T(8,128)S(1)} %bitcast.85, f32[64,128]{1,0:T(8,128)S(1)} %bitcast.89, f32[64,128]{1,0:T(8,128)S(1)} %bitcast.83, ...), kind=kLoop, calls=%fused_computation.20.clone.1 | loop fusion | flops 17801216 | bytes 327680 | tf_op jit(solution)/shard_map/while/body/reduce_sum | solution.py:25
  135.3 0.8 pad_maximum_fusion
  137.0 66.4 %all_to_all.5 = f32[4,6,7,128]{3,2,1,0:T(8,128)S(1)} all-to-all(f32[4,6,7,128]{3,2,1,0:T(8,128)S(1)} %copy.34), channel_id=1, replica_groups=mesh['gx'=4,'gy'=2,'gz'=4] {'gz'}, dimensions={0} | all-to-all | bytes 172032 | tf_op jit(solution)/shard_map/all_to_all | solution.py:116
  (139 shorter events, 30.3 us)
Async XLA Ops:
  0.6 28.3 %copy-start = (s32[1,1024]{1,0:T(1,128)S(1)}, s32[1,1024]{1,0:T(1,128)}, u32[]{:S(2)}) copy-start(s32[1,1024]{1,0:T(1,128)} %param.25) | copy-start | bytes 12292
  0.6 4.0 %copy-start.4 = (s32[12,1]{0,1:T(1,128)S(1)}, s32[12,1]{0,1:T(1,128)}, u32[]{:S(2)}) copy-start(s32[12,1]{0,1:T(1,128)} %param.29) | copy-start | bytes 148
  0.7 4.8 %copy-start.1 = (s32[1,1024]{1,0:T(1,128)S(1)}, s32[1,1024]{1,0:T(1,128)}, u32[]{:S(2)}) copy-start(s32[1,1024]{1,0:T(1,128)} %param.26) | copy-start | bytes 12292
  0.7 9.2 %copy-start.5 = (s32[1,12]{1,0:T(1,128)S(1)}, s32[1,12]{1,0:T(1,128)}, u32[]{:S(2)}) copy-start(s32[1,12]{1,0:T(1,128)} %param.28) | copy-start | bytes 148
  3.0 7.0 %collective-permute-start = (f32[16,4,128]{2,1,0:T(4,128)S(1)}, f32[16,4,128]{2,1,0:T(4,128)S(1)}, u32[]{:S(2)}, u32[]{:S(2)}) collective-permute-start(f32[16,4,128]{2,1,0:T(4,128)S(1)} %gather_fusion.4), channel_id=1, source_target_pairs={{0,8},{8,0},{16,24},{24,16},{1,9},{9,1},{17,25},{25,17},{2,10},{10... | collective-permute-start | bytes 98312 | tf_op jit(solution)/shard_map/ppermute | solution.py:14
  9.9 14.4 %copy-start.2 = (f32[60,4,128]{2,1,0:T(4,128)S(1)}, f32[60,4,128]{2,1,0:T(4,128)}, u32[]{:S(2)}) copy-start(f32[60,4,128]{2,1,0:T(4,128)} %param.22) | copy-start | bytes 368644
  10.6 5.1 %collective-permute-start.1 = (f32[16,4,128]{2,1,0:T(4,128)S(1)}, f32[16,4,128]{2,1,0:T(4,128)S(1)}, u32[]{:S(2)}, u32[]{:S(2)}) collective-permute-start(f32[16,4,128]{2,1,0:T(4,128)S(1)} %gather_fusion.5), channel_id=1, source_target_pairs={{0,16},{8,24},{16,0},{24,8},{1,17},{9,25},{17,1},{25,9},{2,18},{10... | collective-permute-start | bytes 98312 | tf_op jit(solution)/shard_map/ppermute | solution.py:14
  16.3 4.0 %collective-permute-start.2 = (f32[16,4,128]{2,1,0:T(4,128)S(1)}, f32[16,4,128]{2,1,0:T(4,128)S(1)}, u32[]{:S(2)}, u32[]{:S(2)}) collective-permute-start(f32[16,4,128]{2,1,0:T(4,128)S(1)} %gather_fusion.6), channel_id=1, source_target_pairs={{0,4},{4,0},{1,5},{5,1},{2,6},{6,2},{3,7},{7,3},{8,12},{12,8},{9,1... | collective-permute-start | bytes 98312 | tf_op jit(solution)/shard_map/ppermute | solution.py:14
  20.9 1.3 collective-permute-start.3
  22.7 10.7 %collective-permute-start.4 = (f32[16,4,128]{2,1,0:T(4,128)S(1)}, f32[16,4,128]{2,1,0:T(4,128)S(1)}, u32[]{:S(2)}, u32[]{:S(2)}) collective-permute-start(f32[16,4,128]{2,1,0:T(4,128)S(1)} %gather_fusion.8), channel_id=1, source_target_pairs={{0,2},{1,3},{2,0},{3,1},{4,6},{5,7},{6,4},{7,5},{8,10},{9,11},{10,... | collective-permute-start | bytes 98312 | tf_op jit(solution)/shard_map/ppermute | solution.py:14
  33.5 101.7 %copy-start.3 = (f32[60,3,128]{2,0,1:T(8,128)S(1)}, f32[60,3,128]{2,0,1:T(8,128)}, u32[]{:S(2)}) copy-start(f32[60,3,128]{2,0,1:T(8,128)} %param.23) | copy-start | bytes 276484
where the time goes:
time: 204 us
  other arithmetic  89.6 us (44%)
  blocking collectives  66.4 us (33%)
  local copies, waits for them, and re-layouts  29.2 us (14%)
  waiting for transfers between devices  7.28 us (4%)
  starting transfers between devices  6.24 us (3%)
  matrix products  2.94 us (1%)
    reduce_sum x10, other arithmetic, block_forces(): jnp.sum(delta_x * weight, axis=2)  75.9 us
    all_to_all x1, blocking collectives, on_device(): lax.all_to_all(outbox, 'gz', split_axis=0, concat_axis=0, tiled=True)  66.4 us
    ppermute x5, waiting for transfers between devices, swapped(): return lax.ppermute(value, axis, pairs)  7.28 us
    gather x10, local copies, waits for them, and re-layouts, add_group(): bodies[target_rows]  6.57 us
    gather x10, local copies, waits for them, and re-layouts, add_group(): pool_now[source_rows]  6.56 us
    convert_element_type x10, other arithmetic, add_group(): validity = ((offsets >= 0) & (offsets < pair_limit)).astype(jnp.float32)  6.52 us
    ppermute x5, starting transfers between devices, swapped(): return lax.ppermute(value, axis, pairs)  6.24 us
    gather x1, local copies, waits for them, and re-layouts, on_device(): sorted_source = sources[ordering]  4.53 us
  transfers between devices with their start and end apart: 5, of which 3 were waited for; matrix products, arithmetic and copies ran while one was open for 7% of the time, Pallas kernels for 0%

commit v1 on v0

v1 whole, which is shorter than its diff:
```python
import functools

import jax
import jax.numpy as jnp
from jax import lax
from jax.experimental import pallas as pl
from jax.experimental.pallas import tpu as pltpu
from jax.sharding import PartitionSpec as P

soften = 0.01
timestep = 0.25
unroll = 4


def swapped(value, axis, stride):
    mask = 2**stride
    pairs = [(source, source ^ mask) for source in range(lax.axis_size(axis))]
    return lax.ppermute(value, axis, pairs)


def spread(block):
    columns = jnp.concatenate([block, block], axis=0).T
    return [jnp.broadcast_to(columns[:, c : c + 1], (128, 128)) for c in range(4)]


def step_kernel(
    slot_total,
    target_ref,
    source_ref,
    count_ref,
    departures_ref,
    owners_ref,
    pool_ref,
    velocity_ref,
    resident_ref,
    outbox_ref,
    table,
    accel,
    used,
):
    pool_size = pool_ref.shape[0]
    own_blocks = velocity_ref.shape[0]
    span = pool_ref.shape[2]

    @pl.loop(0, pool_size)
    def _(b):
        for c, values in enumerate(spread(pool_ref[b])):
            table[b, c] = values

    accel[...] = jnp.zeros_like(accel)

    @pl.loop(0, (count_ref[0] + unroll - 1) // unroll)
    def _(group):
        for u in range(unroll):
            t = target_ref[group * unroll + u]
            s = source_ref[group * unroll + u]
            xt = jnp.broadcast_to(pool_ref[t, 0:1, :], (8, span))
            yt = jnp.broadcast_to(pool_ref[t, 1:2, :], (8, span))
            zt = jnp.broadcast_to(pool_ref[t, 2:3, :], (8, span))
            ax = ay = az = None
            for g in range(0, span, 8):
                dx = table[s, 0, g : g + 8, :] - xt
                dy = table[s, 1, g : g + 8, :] - yt
                dz = table[s, 2, g : g + 8, :] - zt
                inverse = lax.rsqrt(dx * dx + dy * dy + (dz * dz + soften))
                w = (table[s, 3, g : g + 8, :] * inverse) * (inverse * inverse)
                if ax is None:
                    ax, ay, az = dx * w, dy * w, dz * w
                else:
                    ax, ay, az = ax + dx * w, ay + dy * w, az + dz * w
            accel[t, 0] += ax
            accel[t, 1] += ay
            accel[t, 2] += az

    @pl.loop(0, own_blocks)
    def _(b):
        pull = jnp.sum(accel[b], axis=1)
        velocity_new = velocity_ref[b] + timestep * pull
        block = pool_ref[b]
        resident_ref[b, 0:3, :] = block[0:3] + timestep * velocity_new
        resident_ref[b, 3:4, :] = block[3:4]
        resident_ref[b, 4:7, :] = velocity_new

    outbox_ref[...] = jnp.zeros_like(outbox_ref)
    for g in range(used.shape[0]):
        used[g] = 0
    for m in range(departures_ref.shape[0]):
        d = departures_ref[m]
        owner = owners_ref[m]
        slot = used[owner]
        used[owner] = slot + 1
        outbox_ref[owner * slot_total + slot] = resident_ref[d]
        resident_ref[d] = jnp.zeros(resident_ref.shape[1:], jnp.float32)


def on_device(bodies, velocity, select, pair_target, pair_source, counts, departures, owners):
    own_blocks = bodies.shape[0]
    span = bodies.shape[2]
    pair_total = pair_target.shape[1]
    pool = bodies
    step = 0
    for axis in ("gx", "gy", "gz"):
        for bit in range(lax.axis_size(axis).bit_length() - 1):
            incoming = swapped(pool[select[0, step]], axis, bit)
            pool = jnp.concatenate([pool, incoming], axis=0)
            step += 1
    live = jnp.arange(pair_total, dtype=jnp.int32) < counts[0]
    targets = jnp.where(live, pair_target[0], own_blocks)
    sources = jnp.where(live, pair_source[0], 0)
    group_size = lax.axis_size("gz")
    move_count = departures.shape[1]
    slot_total = max(2, 2 * move_count // group_size)
    smem = pl.BlockSpec(memory_space=pltpu.SMEM)
    vmem = pl.BlockSpec(memory_space=pltpu.VMEM)
    resident, outbox = pl.pallas_call(
        functools.partial(step_kernel, slot_total),
        out_shape=(
            jax.ShapeDtypeStruct((own_blocks, 7, span), jnp.float32),
            jax.ShapeDtypeStruct((group_size * slot_total, 7, span), jnp.float32),
        ),
        in_specs=[smem] * 5 + [vmem] * 2,
        out_specs=(vmem, vmem),
        scratch_shapes=[
            pltpu.VMEM((pool.shape[0], 4, span, span), jnp.float32),
            pltpu.VMEM((own_blocks + 1, 3, 8, span), jnp.float32),
            pltpu.SMEM((group_size,), jnp.int32),
        ],
        compiler_params=pltpu.CompilerParams(vmem_limit_bytes=67043328),
        name="gravity",
    )(targets, sources, counts, departures[0], owners[:, 0], pool, velocity)
    arrived = lax.all_to_all(
        outbox.reshape(group_size, slot_total, 7, span), "gz", split_axis=0, concat_axis=0, tiled=True
    )
    return resident, arrived.reshape(group_size * slot_total, 7, span)


def solution(mesh):
    everywhere = ("gx", "gy", "gz")
    cube = P(everywhere, None, None)
    flat = P(everywhere, None)
    return jax.shard_map(
        on_device,
        mesh=mesh,
        in_specs=(cube, cube, cube, flat, flat, P(everywhere), flat, flat),
        out_specs=(cube, cube),
        check_vma=False,
    )
```

time: 204 us -> 117 us (0.57)
  the two profiles are of different devices: /device:TPU:4 before, /device:TPU:20 now
where the time goes in v1:
time: 117 us; the launch traced here: 116 us
  Pallas kernels  82.7 us (71%)
  local copies, waits for them, and re-layouts  11.6 us (10%)
  waiting for transfers between devices  11 us (9%)
  starting transfers between devices  7.53 us (6%)
  other arithmetic  1.48 us (1%)
  between operations  1.36 us (1%)
    pallas_call x1, Pallas kernels, on_device(): pl.pallas_call(functools.partial(step_kernel, slot_total), out_shape=(jax...  82.7 us
    ppermute x5, waiting for transfers between devices, swapped(): return lax.ppermute(value, axis, pairs)  8.39 us
    unnamed x15, local copies, waits for them, and re-layouts  6.51 us
    ppermute x5, starting transfers between devices, swapped(): return lax.ppermute(value, axis, pairs)  4.23 us
    gather x5, local copies, waits for them, and re-layouts, on_device(): incoming = swapped(pool[select[0, step]], axis, bit)  3.84 us
    all_to_all x1, starting transfers between devices, on_device(): lax.all_to_all(outbox.reshape(group_size, slot_total, 7, span), 'gz', spl...  3.3 us
    all_to_all x1, waiting for transfers between devices, on_device(): lax.all_to_all(outbox.reshape(group_size, slot_total, 7, span), 'gz', spl...  2.59 us
  transfers between devices with their start and end apart: 6, of which 5 were waited for; matrix products, arithmetic and copies ran while one was open for 6% of the time, Pallas kernels for 0%

profile of v1, /device:TPU:20, one launch (start us, length us, event | category | flops | bytes accessed | tf_op | source)
XLA Modules:
  0.0 115.6 jit_solution(6458611880609803584)
XLA Ops:
  0.6 0.7 fusion.6
  1.4 1.5 %gather_fusion = f32[16,4,128]{2,1,0:T(4,128)S(1)} fusion(f32[60,4,128]{2,1,0:T(4,128)} %param.8, s32[1024]{0:T(1024)S(1)} %pad_clamp_fusion.4), kind=kCustom, calls=%fused_computation | custom fusion | bytes 65600 | tf_op jit(solution)/shard_map/gather | solution.py:104
  2.9 1.6 %collective-permute-start = (f32[16,4,128]{2,1,0:T(4,128)S(1)}, f32[16,4,128]{2,1,0:T(4,128)S(1)}, u32[]{:S(2)}, u32[]{:S(2)}) collective-permute-start(f32[16,4,128]{2,1,0:T(4,128)S(1)} %gather_fusion), channel_id=1, source_target_pairs={{0,8},{8,0},{16,24},{24,16},{1,9},{9,1},{17,25},{25,17},{2,10},{10... | collective-permute-start | bytes 98312 | tf_op jit(solution)/shard_map/ppermute | solution.py:18
  4.5 1.6 %constant_dynamic-update-slice_fusion.4 = (f32[124,4,128]{2,1,0:T(4,128)S(1)}, f32[140,4,128]{2,1,0:T(4,128)}) fusion(f32[60,4,128]{2,1,0:T(4,128)} %param.8), kind=kLoop, calls=%fused_computation.12 | loop fusion | bytes 368640
  6.9 0.6 gather_fusion.1
  7.9 0.6 constant_dynamic-update-slice_fusion.3
  8.5 3.9 %collective-permute-done.1 = f32[16,4,128]{2,1,0:T(4,128)S(1)} collective-permute-done((f32[16,4,128]{2,1,0:T(4,128)S(1)}, f32[16,4,128]{2,1,0:T(4,128)S(1)}, u32[]{:S(2)}, u32[]{:S(2)}) %collective-permute-start.1) | collective-permute-done | bytes 32800 | tf_op jit(solution)/shard_map/ppermute | solution.py:18
  12.4 0.6 gather_fusion.2
  13.6 0.6 constant_dynamic-update-slice_fusion.2
  14.2 2.8 %collective-permute-done.2 = f32[16,4,128]{2,1,0:T(4,128)S(1)} collective-permute-done((f32[16,4,128]{2,1,0:T(4,128)S(1)}, f32[16,4,128]{2,1,0:T(4,128)S(1)}, u32[]{:S(2)}, u32[]{:S(2)}) %collective-permute-start.2) | collective-permute-done | bytes 32800 | tf_op jit(solution)/shard_map/ppermute | solution.py:18
  17.0 0.6 gather_fusion.3
  17.7 0.6 constant_dynamic-update-slice_fusion.1
  18.9 0.6 constant_dynamic-update-slice_fusion
  19.5 0.6 gather_fusion.4
  20.1 1.6 %collective-permute-start.4 = (f32[16,4,128]{2,1,0:T(4,128)S(1)}, f32[16,4,128]{2,1,0:T(4,128)S(1)}, u32[]{:S(2)}, u32[]{:S(2)}) collective-permute-start(f32[16,4,128]{2,1,0:T(4,128)S(1)} %gather_fusion.4), channel_id=1, source_target_pairs={{0,2},{1,3},{2,0},{3,1},{4,6},{5,7},{6,4},{7,5},{8,10},{9,11},{10,... | collective-permute-start | bytes 98312 | tf_op jit(solution)/shard_map/ppermute | solution.py:18
  21.7 0.6 fusion
  22.3 0.7 copy.13.velocity_ref
  23.0 1.1 collective-permute-done.4
  24.1 0.6 constant_dynamic-update-slice_fusion.5.pool_ref
  24.7 82.7 %gravity.1 = (f32[60,7,128]{2,1,0:T(8,128)}, f32[24,7,128]{2,1,0:T(8,128)}) custom-call(s32[1024]{0:T(1024)} %get-tuple-element.26.target_ref, s32[1024]{0:T(1024)} %get-tuple-element.25.source_ref, s32[1]{0:T(128)} %copy.25.count_ref, s32[12]{0:T(128)} %bitcast.32, s32[12]{0:T(128)} %bitcast.33, ...), custom_call_target="tpu_custom_call" | custom-call | tf_op jit(solution)/shard_map/gravity/pallas_call | solution.py:115
  107.4 3.3 %all-to-all-start = ((f32[4,6,7,128]{3,2,1,0:T(8,128)}), f32[4,6,7,128]{3,2,1,0:T(8,128)S(1)}, u32[]{:S(2)}, u32[]{:S(2)}) async-start(f32[4,6,7,128]{3,2,1,0:T(8,128)} %bitcast.29), calls=%async_computation | async-start | bytes 196608 | tf_op jit(solution)/shard_map/all_to_all | solution.py:131
  110.7 1.7 %copy.14 = f32[60,7,128]{2,0,1:T(8,128)} copy(f32[60,7,128]{2,1,0:T(8,128)} %get-tuple-element.8) | data formatting | bytes 430080
  112.4 2.6 %all-to-all-done = f32[4,6,7,128]{3,2,1,0:T(8,128)S(1)} async-done(((f32[4,6,7,128]{3,2,1,0:T(8,128)}), f32[4,6,7,128]{3,2,1,0:T(8,128)S(1)}, u32[]{:S(2)}, u32[]{:S(2)}) %all-to-all-start) | async-done | bytes 86048 | tf_op jit(solution)/shard_map/all_to_all | solution.py:131
  115.0 0.7 copy.15
  (21 shorter events, 1.8 us)
Async XLA Ops:
  2.9 4.0 %copy-start = (f32[60,4,128]{2,1,0:T(4,128)S(1)}, f32[60,4,128]{2,1,0:T(4,128)}, u32[]{:S(2)}) copy-start(f32[60,4,128]{2,1,0:T(4,128)} %param.8) | copy-start | bytes 368644
  2.9 4.0 %collective-permute-start = (f32[16,4,128]{2,1,0:T(4,128)S(1)}, f32[16,4,128]{2,1,0:T(4,128)S(1)}, u32[]{:S(2)}, u32[]{:S(2)}) collective-permute-start(f32[16,4,128]{2,1,0:T(4,128)S(1)} %gather_fusion), channel_id=1, source_target_pairs={{0,8},{8,0},{16,24},{24,16},{1,9},{9,1},{17,25},{25,17},{2,10},{10... | collective-permute-start | bytes 98312 | tf_op jit(solution)/shard_map/ppermute | solution.py:18
  7.5 4.9 %collective-permute-start.1 = (f32[16,4,128]{2,1,0:T(4,128)S(1)}, f32[16,4,128]{2,1,0:T(4,128)S(1)}, u32[]{:S(2)}, u32[]{:S(2)}) collective-permute-start(f32[16,4,128]{2,1,0:T(4,128)S(1)} %gather_fusion.1), channel_id=1, source_target_pairs={{0,16},{8,24},{16,0},{24,8},{1,17},{9,25},{17,1},{25,9},{2,18},{10... | collective-permute-start | bytes 98312 | tf_op jit(solution)/shard_map/ppermute | solution.py:18
  13.0 4.0 %collective-permute-start.2 = (f32[16,4,128]{2,1,0:T(4,128)S(1)}, f32[16,4,128]{2,1,0:T(4,128)S(1)}, u32[]{:S(2)}, u32[]{:S(2)}) collective-permute-start(f32[16,4,128]{2,1,0:T(4,128)S(1)} %gather_fusion.2), channel_id=1, source_target_pairs={{0,4},{4,0},{1,5},{5,1},{2,6},{6,2},{3,7},{7,3},{8,12},{12,8},{9,1... | collective-permute-start | bytes 98312 | tf_op jit(solution)/shard_map/ppermute | solution.py:18
  17.6 1.3 %collective-permute-start.3 = (f32[16,4,128]{2,1,0:T(4,128)S(1)}, f32[16,4,128]{2,1,0:T(4,128)S(1)}, u32[]{:S(2)}, u32[]{:S(2)}) collective-permute-start(f32[16,4,128]{2,1,0:T(4,128)S(1)} %gather_fusion.3), channel_id=1, source_target_pairs={{0,1},{1,0},{2,3},{3,2},{4,5},{5,4},{6,7},{7,6},{8,9},{9,8},{10,11... | collective-permute-start | bytes 98312 | tf_op jit(solution)/shard_map/ppermute | solution.py:18
  18.3 4.0 %copy-start.1 = (f32[60,3,128]{2,0,1:T(8,128)S(1)}, f32[60,3,128]{2,0,1:T(8,128)}, u32[]{:S(2)}) copy-start(f32[60,3,128]{2,0,1:T(8,128)} %param.9) | copy-start | bytes 276484
  19.5 2.2 %copy-start.3 = (s32[1,1024]{1,0:T(1,128)S(1)}, s32[1,1024]{1,0:T(1,128)}, u32[]{:S(2)}) copy-start(s32[1,1024]{1,0:T(1,128)} %param.11) | copy-start | bytes 12292
  20.1 1.6 %copy-start.2 = (s32[1,1024]{1,0:T(1,128)S(1)}, s32[1,1024]{1,0:T(1,128)}, u32[]{:S(2)}) copy-start(s32[1,1024]{1,0:T(1,128)} %param.12) | copy-start | bytes 12292
  20.1 4.0 %collective-permute-start.4 = (f32[16,4,128]{2,1,0:T(4,128)S(1)}, f32[16,4,128]{2,1,0:T(4,128)S(1)}, u32[]{:S(2)}, u32[]{:S(2)}) collective-permute-start(f32[16,4,128]{2,1,0:T(4,128)S(1)} %gather_fusion.4), channel_id=1, source_target_pairs={{0,2},{1,3},{2,0},{3,1},{4,6},{5,7},{6,4},{7,5},{8,10},{9,11},{10,... | collective-permute-start | bytes 98312 | tf_op jit(solution)/shard_map/ppermute | solution.py:18
  107.4 7.6 %all-to-all-start = ((f32[4,6,7,128]{3,2,1,0:T(8,128)}), f32[4,6,7,128]{3,2,1,0:T(8,128)S(1)}, u32[]{:S(2)}, u32[]{:S(2)}) async-start(f32[4,6,7,128]{3,2,1,0:T(8,128)} %bitcast.29), calls=%async_computation | async-start | bytes 196608 | tf_op jit(solution)/shard_map/all_to_all | solution.py:131

commit v2 on v1

--- a/solution.py
+++ b/solution.py
@@ -1,4 +1,5 @@
 import functools
+import math
 
 import jax
 import jax.numpy as jnp
@@ -9,7 +10,7 @@
 
 soften = 0.01
 timestep = 0.25
-unroll = 4
+deepest_unroll = 16
 
 
 def swapped(value, axis, stride):
@@ -18,9 +19,11 @@
     return lax.ppermute(value, axis, pairs)
 
 
-def spread(block):
-    columns = jnp.concatenate([block, block], axis=0).T
-    return [jnp.broadcast_to(columns[:, c : c + 1], (128, 128)) for c in range(4)]
+def split(values):
+    high = jnp.clip(values, -3.38e38, 3.38e38).astype(jnp.bfloat16).astype(jnp.float32)
+    rest = values - high
+    middle = rest.astype(jnp.bfloat16).astype(jnp.float32)
+    return high, middle, rest - middle
 
 
 def step_kernel(
@@ -34,18 +37,35 @@
     velocity_ref,
     resident_ref,
     outbox_ref,
-    table,
+    sources,
+    targets,
     accel,
     used,
 ):
     pool_size = pool_ref.shape[0]
     own_blocks = velocity_ref.shape[0]
     span = pool_ref.shape[2]
+    unroll = math.gcd(target_ref.shape[0], deepest_unroll)
+
+    row = lax.broadcasted_iota(jnp.int32, (12, 4 * span), 0)
+    lane = lax.broadcasted_iota(jnp.int32, (12, 4 * span), 1)
+    picks = (row % 4 == lane // span).astype(jnp.float32)
+    ones = (lax.broadcasted_iota(jnp.int32, (4, span), 0) < 3).astype(jnp.float32)
 
     @pl.loop(0, pool_size)
     def _(b):
-        for c, values in enumerate(spread(pool_ref[b])):
-            table[b, c] = values
+        pieces = split(pool_ref[b])
+        sources[b] = jnp.concatenate([*pieces, ones], axis=0).T.astype(jnp.bfloat16)
+
+    @pl.loop(0, own_blocks + 1)
+    def _(b):
+        nothing = jnp.zeros((1, span), jnp.float32)
+        rows = [
+            jnp.concatenate([-piece[0:1], -piece[1:2], -piece[2:3], nothing], axis=1)
+            for piece in split(pool_ref[b])
+        ]
+        rows.append(jnp.zeros((1, 4 * span), jnp.float32))
+        targets[b] = jnp.concatenate([picks, *rows], axis=0).astype(jnp.bfloat16)
 
     accel[...] = jnp.zeros_like(accel)
 
@@ -54,16 +74,15 @@
         for u in range(unroll):
             t = target_ref[group * unroll + u]
             s = source_ref[group * unroll + u]
-            xt = jnp.broadcast_to(pool_ref[t, 0:1, :], (8, span))
-            yt = jnp.broadcast_to(pool_ref[t, 1:2, :], (8, span))
-            zt = jnp.broadcast_to(pool_ref[t, 2:3, :], (8, span))
+            gaps = jnp.dot(sources[s], targets[t], preferred_element_type=jnp.float32)
             ax = ay = az = None
             for g in range(0, span, 8):
-                dx = table[s, 0, g : g + 8, :] - xt
-                dy = table[s, 1, g : g + 8, :] - yt
-                dz = table[s, 2, g : g + 8, :] - zt
+                dx = gaps[g : g + 8, 0:span]
+                dy = gaps[g : g + 8, span : 2 * span]
+                dz = gaps[g : g + 8, 2 * span : 3 * span]
+                mass = gaps[g : g + 8, 3 * span :]
                 inverse = lax.rsqrt(dx * dx + dy * dy + (dz * dz + soften))
-                w = (table[s, 3, g : g + 8, :] * inverse) * (inverse * inverse)
+                w = (mass * inverse) * (inverse * inverse)
                 if ax is None:
                     ax, ay, az = dx * w, dy * w, dz * w
                 else:
@@ -121,11 +140,11 @@
         in_specs=[smem] * 5 + [vmem] * 2,
         out_specs=(vmem, vmem),
         scratch_shapes=[
-            pltpu.VMEM((pool.shape[0], 4, span, span), jnp.float32),
+            pltpu.VMEM((pool.shape[0], span, 16), jnp.bfloat16),
+            pltpu.VMEM((own_blocks + 1, 16, 4 * span), jnp.bfloat16),
             pltpu.VMEM((own_blocks + 1, 3, 8, span), jnp.float32),
             pltpu.SMEM((group_size,), jnp.int32),
         ],
-        compiler_params=pltpu.CompilerParams(vmem_limit_bytes=67043328),
         name="gravity",
     )(targets, sources, counts, departures[0], owners[:, 0], pool, velocity)
     arrived = lax.all_to_all(

time: 117 us -> 96.1 us (0.82)
  the two profiles are of different devices: /device:TPU:20 before, /device:TPU:0 now
where the time goes in v2:
time: 96.1 us; the launch traced here: 95.1 us
  Pallas kernels  39.3 us (41%)
  starting transfers between devices  35.6 us (37%)
  waiting for transfers between devices  8.74 us (9%)
  local copies, waits for them, and re-layouts  8.62 us (9%)
  other arithmetic  1.48 us (2%)
  between operations  1.38 us (1%)
    pallas_call x1, Pallas kernels, on_device(): pl.pallas_call(functools.partial(step_kernel, slot_total), out_shape=(jax...  39.3 us
    all_to_all x1, starting transfers between devices, on_device(): lax.all_to_all(outbox.reshape(group_size, slot_total, 7, span), 'gz', spl...  25.5 us
    ppermute x5, starting transfers between devices, swapped(): return lax.ppermute(value, axis, pairs)  10.1 us
    ppermute x5, waiting for transfers between devices, swapped(): return lax.ppermute(value, axis, pairs)  6.11 us
    unnamed x17, local copies, waits for them, and re-layouts  4.75 us
    gather x5, local copies, waits for them, and re-layouts, on_device(): incoming = swapped(pool[select[0, step]], axis, bit)  3.84 us
    all_to_all x1, waiting for transfers between devices, on_device(): lax.all_to_all(outbox.reshape(group_size, slot_total, 7, span), 'gz', spl...  2.62 us
  transfers between devices with their start and end apart: 6, of which 6 were waited for; matrix products, arithmetic and copies ran while one was open for 4% of the time, Pallas kernels for 0%

profile of v2, /device:TPU:0, one launch (start us, length us, event | category | flops | bytes accessed | tf_op | source)
XLA Modules:
  0.0 95.1 jit_solution(17799317329366780763)
XLA Ops:
  0.6 0.7 fusion.6
  1.4 1.5 %gather_fusion = f32[16,4,128]{2,1,0:T(4,128)S(1)} fusion(f32[60,4,128]{2,1,0:T(4,128)} %param.8, s32[1024]{0:T(1024)S(1)} %pad_clamp_fusion.4), kind=kCustom, calls=%fused_computation | custom fusion | bytes 65600 | tf_op jit(solution)/shard_map/gather | solution.py:123
  2.9 3.1 %collective-permute-start = (f32[16,4,128]{2,1,0:T(4,128)S(1)}, f32[16,4,128]{2,1,0:T(4,128)S(1)}, u32[]{:S(2)}, u32[]{:S(2)}) collective-permute-start(f32[16,4,128]{2,1,0:T(4,128)S(1)} %gather_fusion), channel_id=1, source_target_pairs={{0,8},{8,0},{16,24},{24,16},{1,9},{9,1},{17,25},{25,17},{2,10},{10... | collective-permute-start | bytes 98312 | tf_op jit(solution)/shard_map/ppermute | solution.py:19
  6.0 0.9 constant_dynamic-update-slice_fusion.4
  7.6 0.3 collective-permute-done
  7.9 0.6 gather_fusion.1
  8.5 3.1 %collective-permute-start.1 = (f32[16,4,128]{2,1,0:T(4,128)S(1)}, f32[16,4,128]{2,1,0:T(4,128)S(1)}, u32[]{:S(2)}, u32[]{:S(2)}) collective-permute-start(f32[16,4,128]{2,1,0:T(4,128)S(1)} %gather_fusion.1), channel_id=1, source_target_pairs={{0,16},{8,24},{16,0},{24,8},{1,17},{9,25},{17,1},{25,9},{2,18},{10... | collective-permute-start | bytes 98312 | tf_op jit(solution)/shard_map/ppermute | solution.py:19
  11.6 1.9 %collective-permute-done.1 = f32[16,4,128]{2,1,0:T(4,128)S(1)} collective-permute-done((f32[16,4,128]{2,1,0:T(4,128)S(1)}, f32[16,4,128]{2,1,0:T(4,128)S(1)}, u32[]{:S(2)}, u32[]{:S(2)}) %collective-permute-start.1) | collective-permute-done | bytes 32800 | tf_op jit(solution)/shard_map/ppermute | solution.py:19
  13.5 0.6 gather_fusion.2
  14.1 1.9 %collective-permute-start.2 = (f32[16,4,128]{2,1,0:T(4,128)S(1)}, f32[16,4,128]{2,1,0:T(4,128)S(1)}, u32[]{:S(2)}, u32[]{:S(2)}) collective-permute-start(f32[16,4,128]{2,1,0:T(4,128)S(1)} %gather_fusion.2), channel_id=1, source_target_pairs={{0,4},{4,0},{1,5},{5,1},{2,6},{6,2},{3,7},{7,3},{8,12},{12,8},{9,1... | collective-permute-start | bytes 98312 | tf_op jit(solution)/shard_map/ppermute | solution.py:19
  16.1 2.0 %collective-permute-done.2 = f32[16,4,128]{2,1,0:T(4,128)S(1)} collective-permute-done((f32[16,4,128]{2,1,0:T(4,128)S(1)}, f32[16,4,128]{2,1,0:T(4,128)S(1)}, u32[]{:S(2)}, u32[]{:S(2)}) %collective-permute-start.2) | collective-permute-done | bytes 32800 | tf_op jit(solution)/shard_map/ppermute | solution.py:19
  18.2 0.6 gather_fusion.3
  18.9 1.2 %collective-permute-done.3 = f32[16,4,128]{2,1,0:T(4,128)S(1)} collective-permute-done((f32[16,4,128]{2,1,0:T(4,128)S(1)}, f32[16,4,128]{2,1,0:T(4,128)S(1)}, u32[]{:S(2)}, u32[]{:S(2)}) %collective-permute-start.3) | collective-permute-done | bytes 32800 | tf_op jit(solution)/shard_map/ppermute | solution.py:19
  20.1 0.6 gather_fusion.4
  20.6 1.9 %collective-permute-start.4 = (f32[16,4,128]{2,1,0:T(4,128)S(1)}, f32[16,4,128]{2,1,0:T(4,128)S(1)}, u32[]{:S(2)}, u32[]{:S(2)}) collective-permute-start(f32[16,4,128]{2,1,0:T(4,128)S(1)} %gather_fusion.4), channel_id=1, source_target_pairs={{0,2},{1,3},{2,0},{3,1},{4,6},{5,7},{6,4},{7,5},{8,10},{9,11},{10,... | collective-permute-start | bytes 98312 | tf_op jit(solution)/shard_map/ppermute | solution.py:19
  22.5 0.6 fusion
  23.1 0.7 copy.13.velocity_ref
  23.9 0.8 collective-permute-done.4
  24.6 0.7 copy-done.1
  25.3 39.3 %gravity.1 = (f32[60,7,128]{2,1,0:T(8,128)}, f32[24,7,128]{2,1,0:T(8,128)}) custom-call(s32[1024]{0:T(1024)} %get-tuple-element.26.target_ref, s32[1024]{0:T(1024)} %get-tuple-element.25.source_ref, s32[1]{0:T(128)} %copy.25.count_ref, s32[12]{0:T(128)} %bitcast.32, s32[12]{0:T(128)} %bitcast.33, f32[140,4,128]{2,1,0:T(4,128)} %copy-done.1, ...), custom_call_target="tpu_custom_call" | custom-call | tf_op jit(solution)/shard_map/gravity/pallas_call | solution.py:134
  64.7 25.5 %all-to-all-start = ((f32[4,6,7,128]{3,2,1,0:T(8,128)}), f32[4,6,7,128]{3,2,1,0:T(8,128)S(1)}, u32[]{:S(2)}, u32[]{:S(2)}) async-start(f32[4,6,7,128]{3,2,1,0:T(8,128)} %bitcast.29), calls=%async_computation | async-start | bytes 196608 | tf_op jit(solution)/shard_map/all_to_all | solution.py:150
  90.2 1.7 %copy.14 = f32[60,7,128]{2,0,1:T(8,128)} copy(f32[60,7,128]{2,1,0:T(8,128)} %get-tuple-element.8) | data formatting | bytes 430080
  91.9 2.6 %all-to-all-done = f32[4,6,7,128]{3,2,1,0:T(8,128)S(1)} async-done(((f32[4,6,7,128]{3,2,1,0:T(8,128)}), f32[4,6,7,128]{3,2,1,0:T(8,128)S(1)}, u32[]{:S(2)}, u32[]{:S(2)}) %all-to-all-start) | async-done | bytes 86048 | tf_op jit(solution)/shard_map/all_to_all | solution.py:150
  94.5 0.7 copy.15
  (23 shorter events, 0.3 us)
Async XLA Ops:
  2.9 5.0 %copy-start = (f32[60,4,128]{2,1,0:T(4,128)S(1)}, f32[60,4,128]{2,1,0:T(4,128)}, u32[]{:S(2)}) copy-start(f32[60,4,128]{2,1,0:T(4,128)} %param.8) | copy-start | bytes 368644
  2.9 5.0 %collective-permute-start = (f32[16,4,128]{2,1,0:T(4,128)S(1)}, f32[16,4,128]{2,1,0:T(4,128)S(1)}, u32[]{:S(2)}, u32[]{:S(2)}) collective-permute-start(f32[16,4,128]{2,1,0:T(4,128)S(1)} %gather_fusion), channel_id=1, source_target_pairs={{0,8},{8,0},{16,24},{24,16},{1,9},{9,1},{17,25},{25,17},{2,10},{10... | collective-permute-start | bytes 98312 | tf_op jit(solution)/shard_map/ppermute | solution.py:19
  8.5 5.0 %collective-permute-start.1 = (f32[16,4,128]{2,1,0:T(4,128)S(1)}, f32[16,4,128]{2,1,0:T(4,128)S(1)}, u32[]{:S(2)}, u32[]{:S(2)}) collective-permute-start(f32[16,4,128]{2,1,0:T(4,128)S(1)} %gather_fusion.1), channel_id=1, source_target_pairs={{0,16},{8,24},{16,0},{24,8},{1,17},{9,25},{17,1},{25,9},{2,18},{10... | collective-permute-start | bytes 98312 | tf_op jit(solution)/shard_map/ppermute | solution.py:19
  14.1 4.0 %collective-permute-start.2 = (f32[16,4,128]{2,1,0:T(4,128)S(1)}, f32[16,4,128]{2,1,0:T(4,128)S(1)}, u32[]{:S(2)}, u32[]{:S(2)}) collective-permute-start(f32[16,4,128]{2,1,0:T(4,128)S(1)} %gather_fusion.2), channel_id=1, source_target_pairs={{0,4},{4,0},{1,5},{5,1},{2,6},{6,2},{3,7},{7,3},{8,12},{12,8},{9,1... | collective-permute-start | bytes 98312 | tf_op jit(solution)/shard_map/ppermute | solution.py:19
  18.8 1.3 %collective-permute-start.3 = (f32[16,4,128]{2,1,0:T(4,128)S(1)}, f32[16,4,128]{2,1,0:T(4,128)S(1)}, u32[]{:S(2)}, u32[]{:S(2)}) collective-permute-start(f32[16,4,128]{2,1,0:T(4,128)S(1)} %gather_fusion.3), channel_id=1, source_target_pairs={{0,1},{1,0},{2,3},{3,2},{4,5},{5,4},{6,7},{7,6},{8,9},{9,8},{10,11... | collective-permute-start | bytes 98312 | tf_op jit(solution)/shard_map/ppermute | solution.py:19
  18.9 4.3 %copy-start.2 = (f32[60,3,128]{2,0,1:T(8,128)S(1)}, f32[60,3,128]{2,0,1:T(8,128)}, u32[]{:S(2)}) copy-start(f32[60,3,128]{2,0,1:T(8,128)} %param.9) | copy-start | bytes 276484
  20.0 2.5 %copy-start.4 = (s32[1,1024]{1,0:T(1,128)S(1)}, s32[1,1024]{1,0:T(1,128)}, u32[]{:S(2)}) copy-start(s32[1,1024]{1,0:T(1,128)} %param.11) | copy-start | bytes 12292
  20.6 1.9 %copy-start.3 = (s32[1,1024]{1,0:T(1,128)S(1)}, s32[1,1024]{1,0:T(1,128)}, u32[]{:S(2)}) copy-start(s32[1,1024]{1,0:T(1,128)} %param.12) | copy-start | bytes 12292
  20.6 4.0 %collective-permute-start.4 = (f32[16,4,128]{2,1,0:T(4,128)S(1)}, f32[16,4,128]{2,1,0:T(4,128)S(1)}, u32[]{:S(2)}, u32[]{:S(2)}) collective-permute-start(f32[16,4,128]{2,1,0:T(4,128)S(1)} %gather_fusion.4), channel_id=1, source_target_pairs={{0,2},{1,3},{2,0},{3,1},{4,6},{5,7},{6,4},{7,5},{8,10},{9,11},{10,... | collective-permute-start | bytes 98312 | tf_op jit(solution)/shard_map/ppermute | solution.py:19
  24.6 0.7 copy-start.1
  64.7 29.8 %all-to-all-start = ((f32[4,6,7,128]{3,2,1,0:T(8,128)}), f32[4,6,7,128]{3,2,1,0:T(8,128)S(1)}, u32[]{:S(2)}, u32[]{:S(2)}) async-start(f32[4,6,7,128]{3,2,1,0:T(8,128)} %bitcast.29), calls=%async_computation | async-start | bytes 196608 | tf_op jit(solution)/shard_map/all_to_all | solution.py:150
